TPU v7x, 32 devices: a whole 2x2x4 slice. The times are simulated.
32 devices in a mesh: expert: 8 (over y, x, core), dp: 4 (over z).
Axes of the slice: x: 2, y: 2, z: 4, core: 2. Of those that a mesh axis runs over, the one named last changes fastest.
Arguments:
- trunk: bfloat16 [768, 4096], P(('dp', 'expert')), may hold values from -6 to 6
- w_first: bfloat16 [8, 4096, 2048], P('expert'), may hold values from -0.09375 to 0.09375
- w_second: bfloat16 [8, 2048, 1024], P('expert'), may hold values from -0.125 to 0.125
- gates: bfloat16 [8, 8, 768], P('expert', None, 'dp'), may hold values from 0.049804688 to 1
- d_mixed: bfloat16 [768, 8, 1024], P(('dp', 'expert')), may hold values from -6 to 6
Outputs:
- mixed: bfloat16 [768, 8, 1024], P(('dp', 'expert'))
- d_trunk: bfloat16 [768, 4096], P(('dp', 'expert'))
- d_gates: bfloat16 [8, 8, 768], P('expert', None, 'dp')
- d_w_first: bfloat16 [8, 4096, 2048], P('expert', 'dp')
- d_w_second: bfloat16 [8, 2048, 1024], P('expert', 'dp')
All inputs are finite; a program needn't handle non-finite values.
Results may differ from a plain program's by a relative error of at most 0.015.
Values may be sent and summed in bfloat16 or wider, within the bound.
A program may use at most 128 MiB of HBM per device.

v0:
```python
import jax
import jax.numpy as jnp
from jax import lax
from jax.sharding import PartitionSpec as P


def on_device(trunk, w_first, w_second, gates, d_mixed):
    rows_all = lax.all_gather(trunk, "expert", axis=0, tiled=True)
    first = w_first[0]
    second = w_second[0]
    gate_here = gates[0]
    pre = jnp.dot(rows_all, first, preferred_element_type=jnp.float32)
    hidden = jax.nn.silu(pre).astype(jnp.bfloat16)
    output = jnp.dot(hidden, second, preferred_element_type=jnp.float32).astype(jnp.bfloat16)
    outs_each, gates_each = (
        lax.all_to_all(output[None], "expert", split_axis=1, concat_axis=0, tiled=True),
        lax.all_to_all(gate_here.T[None], "expert", split_axis=1, concat_axis=0, tiled=True),
    )
    mixed = jnp.einsum(
        "ert,ero->rto", gates_each, outs_each, preferred_element_type=jnp.float32
    ).astype(jnp.bfloat16)
    d_out_each = jnp.einsum(
        "ert,rto->ero", gates_each, d_mixed, preferred_element_type=jnp.float32
    ).astype(jnp.bfloat16)
    d_gate_each = jnp.einsum(
        "rto,ero->ert", d_mixed, outs_each, preferred_element_type=jnp.float32
    ).astype(jnp.bfloat16)
    back_out, back_gate = (
        lax.all_to_all(d_out_each, "expert", split_axis=0, concat_axis=1, tiled=True),
        lax.all_to_all(d_gate_each, "expert", split_axis=0, concat_axis=1, tiled=True),
    )
    d_output = back_out[0]
    d_gate = back_gate[0].T[None]
    d_hidden = lax.dot_general(
        d_output, second, (((1,), (1,)), ((), ())), preferred_element_type=jnp.float32
    )
    sig = jax.nn.sigmoid(pre)
    d_pre = (d_hidden * sig * (1.0 + pre * (1.0 - sig))).astype(jnp.bfloat16)
    piece = d_pre
    d_trunk = lax.psum_scatter(
        lax.dot_general(
            piece, first, (((1,), (1,)), ((), ())), preferred_element_type=jnp.float32
        ).astype(jnp.bfloat16),
        "expert",
        scatter_dimension=0,
        tiled=True,
    )
    piece = rows_all
    d_first = lax.psum_scatter(
        lax.dot_general(
            piece, d_pre, (((0,), (0,)), ((), ())), preferred_element_type=jnp.float32
        ).astype(jnp.bfloat16),
        "dp",
        scatter_dimension=0,
        tiled=True,
    )
    piece = hidden
    d_second = lax.psum_scatter(
        lax.dot_general(
            piece, d_output, (((0,), (0,)), ((), ())), preferred_element_type=jnp.float32
        ).astype(jnp.bfloat16),
        "dp",
        scatter_dimension=0,
        tiled=True,
    )
    return (mixed, d_trunk, d_gate, d_first[None], d_second[None])


def solution(mesh):
    in_specs = (
        P(("dp", "expert"), None),
        P("expert", None, None),
        P("expert", None, None),
        P("expert", None, "dp"),
        P(("dp", "expert"), None, None),
    )
    out_specs = (
        P(("dp", "expert"), None, None),
        P(("dp", "expert"), None),
        P("expert", None, "dp"),
        P("expert", "dp", None),
        P("expert", "dp", None),
    )
    return jax.shard_map(
        on_device, mesh=mesh, in_specs=in_specs, out_specs=out_specs, check_vma=False
    )
```

profile of v0, /device:TPU:0, one launch (start us, length us, event | category | flops | bytes accessed | tf_op | source)
XLA Modules:
  0.0 471.3 jit_solution(6701005433292984852)
XLA Ops:
  7.2 0.7 all-gather.2.cloned.1.call-update
  7.9 0.8 copy.31
  8.7 10.2 %all_to_all.42 = bf16[1,192,8]{2,0,1:T(2,128)(2,1)S(1)} all-to-all(bf16[1,192,8]{2,0,1:T(2,128)(2,1)S(1)} %copy.31), channel_id=1, replica_groups=mesh['expert'=8,'dp'=4] {'expert'}, dimensions={1} | all-to-all | bytes 6144 | tf_op jit(solution)/shard_map/all_to_all | solution.py:17
  19.2 0.2 fusion.24
  19.5 1.0 copy.36
  20.5 3.5 all-to-all-start.2
  24.0 14.2 %all-gather.2.cloned.1.call-done = bf16[192,4096]{1,0:T(8,128)(2,1)} async-done(((bf16[24,4096]{1,0:T(8,128)(2,1)}), bf16[192,4096]{1,0:T(8,128)(2,1)}) %all-gather.2.cloned.1.call-update) | async-done | bytes 1572880 | tf_op jit(solution)/shard_map/all_gather | solution.py:8
  38.2 10.8 %fusion.2 = f32[192,2048]{1,0:T(8,128)} fusion(bf16[192,4096]{1,0:T(8,128)(2,1)} %all-gather.2.cloned.1.call-done, bf16[1,4096,2048]{2,1,0:T(8,128)(2,1)} %param.6), kind=kOutput, calls=%fused_computation.2 | convolution fusion | flops 3221225472 | bytes 19922944 | tf_op jit(solution)/shard_map/dot_general | solution.py:12
  49.0 4.5 fusion.17
  53.6 8.1 %convert_bitcast_fusion = bf16[4096,2048]{0,1:T(8,128)(2,1)} fusion(bf16[192,2048]{1,0:T(8,128)(2,1)S(1)} %fusion.17, bf16[192,4096]{1,0:T(8,128)(2,1)S(1)} %copy-done.1), kind=kOutput, calls=%fused_computation.4 | convolution fusion | flops 3229614080 | bytes 19136512 | tf_op jit(solution)/shard_map/dot_general | solution.py:50
  61.8 12.6 %fusion.4 = bf16[192,4096]{1,0:T(8,128)(2,1)} fusion(bf16[192,2048]{1,0:T(8,128)(2,1)S(1)} %fusion.17, bf16[1,4096,2048]{2,1,0:T(8,128)(2,1)} %param.6), kind=kOutput, calls=%fused_computation.5 | convolution fusion | flops 3222011904 | bytes 19136512 | tf_op jit(solution)/shard_map/dot_general | solution.py:41
  74.4 0.2 reduce-scatter.8.cloned.1.call-start
  74.6 1.2 copy-done.2
  75.8 3.3 convolution_convert_fusion
  79.1 3.2 fusion.25
  82.3 0.6 copy.47
  83.0 0.5 broadcast.1
  83.5 2.9 reduce
  86.4 0.2 reshape.24
  86.7 10.8 %all_to_all.43 = bf16[8,2,12288]{2,1,0:T(2,128)(2,1)S(1)} all-to-all(bf16[8,2,12288]{2,1,0:T(2,128)(2,1)S(1)} %reshape.24), channel_id=1, replica_groups=mesh['expert'=8,'dp'=4] {'expert'}, dimensions={0} | all-to-all | bytes 786432 | tf_op jit(solution)/shard_map/all_to_all | solution.py:16
  97.5 0.4 reshape.25
  97.9 0.1 copy.41
  98.0 0.4 fusion.28
  98.4 0.7 copy.38
  99.1 3.3 all-to-all-start.3
  102.5 1.1 fusion.23
  103.6 3.6 all-to-all-done.3
  107.1 0.7 squeeze.19
  107.8 234.5 %reduce-scatter.6.cloned.1.call-done = bf16[1024,2048]{0,1:T(8,128)(2,1)} async-done(((bf16[4096,2048]{0,1:T(8,128)(2,1)}), bf16[1024,2048]{0,1:T(8,128)(2,1)}) %reduce-scatter.6.cloned.1.call-update) | async-done | bytes 4194320 | tf_op jit(solution)/shard_map/reduce_scatter | solution.py:49
  342.3 6.4 %copy.40 = bf16[1,1024,2048]{2,1,0:T(8,128)(2,1)} copy(bf16[1,1024,2048]{1,2,0:T(8,128)(2,1)} %bitcast.62) | data formatting | bytes 8388608
  348.7 36.4 %reduce-scatter.4.cloned.1.call-done = bf16[24,4096]{1,0:T(8,128)(2,1)} async-done(((bf16[192,4096]{1,0:T(8,128)(2,1)}), bf16[24,4096]{1,0:T(8,128)(2,1)}) %reduce-scatter.4.cloned.1.call-update) | async-done | bytes 196624 | tf_op jit(solution)/shard_map/reduce_scatter | solution.py:40
  385.2 79.6 %reduce-scatter.8.cloned.1.call-done = bf16[512,1024]{1,0:T(8,128)(2,1)} async-done(((bf16[2048,1024]{1,0:T(8,128)(2,1)}), bf16[512,1024]{1,0:T(8,128)(2,1)}) %reduce-scatter.8.cloned.1.call-update) | async-done | bytes 1048592 | tf_op jit(solution)/shard_map/reduce_scatter | solution.py:58
  (16 shorter events, 0.5 us)
Async XLA Ops:
  7.2 12.1 %copy-start = (bf16[24,8,1024]{2,1,0:T(8,128)(2,1)S(1)}, bf16[24,8,1024]{2,1,0:T(8,128)(2,1)}, u32[]{:S(2)}) copy-start(bf16[24,8,1024]{2,1,0:T(8,128)(2,1)} %param.9) | copy-start | bytes 1179652
  7.2 31.0 %all-gather.2.cloned.1.call-start = ((), (), s32[]{:S(2)}) async-start(), calls=%async_computation.7 | async-start | bytes 1769472 | tf_op jit(solution)/shard_map/all_gather | solution.py:8
  20.5 28.6 %all-to-all-start.2 = ((bf16[8,24,1024]{2,1,0:T(8,128)(2,1)}), bf16[8,24,1024]{2,1,0:T(8,128)(2,1)S(1)}, u32[]{:S(2)}, u32[]{:S(2)}) async-start(bf16[8,24,1024]{2,1,0:T(8,128)(2,1)} %copy.36), calls=%async_computation.2 | async-start | bytes 786432 | tf_op jit(solution)/shard_map/all_to_all | solution.py:29
  23.9 318.4 %reduce-scatter.6.cloned.1.call-start = ((), (), s32[]{:S(2)}) async-start(), calls=%async_computation.9 | async-start | bytes 20971520 | tf_op jit(solution)/shard_map/reduce_scatter | solution.py:49
  49.0 4.5 copy-start.1
  61.7 323.5 %reduce-scatter.4.cloned.1.call-start = ((), (), s32[]{:S(2)}) async-start(), calls=%async_computation.8 | async-start | bytes 1769472 | tf_op jit(solution)/shard_map/reduce_scatter | solution.py:40
  74.4 1.4 copy-start.2
  74.4 390.3 %reduce-scatter.8.cloned.1.call-start = ((), (), s32[]{:S(2)}) async-start(), calls=%async_computation.10 | async-start | bytes 5242880 | tf_op jit(solution)/shard_map/reduce_scatter | solution.py:58
  99.1 8.0 %all-to-all-start.3 = ((bf16[8,24,8]{1,2,0:T(8,128)(2,1)}), bf16[8,24,8]{1,2,0:T(8,128)(2,1)S(1)}, u32[]{:S(2)}, u32[]{:S(2)}) async-start(bf16[8,24,8]{1,2,0:T(8,128)(2,1)} %copy.38), calls=%async_computation.4 | async-start | bytes 32768 | tf_op jit(solution)/shard_map/all_to_all | solution.py:30
Sparse Core Ops, SparseCore 0:
  9.9 28.2 all-gather.1
  61.8 280.4 reduce-scatter.5
  346.2 38.9 reduce-scatter.3
  387.9 76.7 reduce-scatter.7
where the time goes:
time: 472 us; the launch traced here: 471 us
  waiting for transfers between devices  369 us (78%)
  matrix products  44.3 us (9%)
  blocking collectives  21 us (4%)
  between operations  13.9 us (3%)
  local copies, waits for them, and re-layouts  12.9 us (3%)
  starting transfers between devices  7.13 us (2%)
    reduce_scatter x1, waiting for transfers between devices, on_device(): lax.psum_scatter(lax.dot_general(piece, d_pre, (((0,), (0,)), ((), ())),...  234 us
    reduce_scatter x1, waiting for transfers between devices, on_device(): lax.psum_scatter(lax.dot_general(piece, d_output, (((0,), (0,)), ((), ())...  79.6 us
    reduce_scatter x1, waiting for transfers between devices, on_device(): lax.psum_scatter(lax.dot_general(piece, first, (((1,), (1,)), ((), ())),...  36.4 us
    all_gather x1, waiting for transfers between devices, on_device(): rows_all = lax.all_gather(trunk, 'expert', axis=0, tiled=True)  14.2 us
    dot_general x1, matrix products, on_device(): lax.dot_general(piece, first, (((1,), (1,)), ((), ())), preferred_element...  12.6 us
    all_to_all x1, blocking collectives, on_device(): lax.all_to_all(output[None], 'expert', split_axis=1, concat_axis=0, tiled...  10.8 us
    dot_general x1, matrix products, on_device(): pre = jnp.dot(rows_all, first, preferred_element_type=jnp.float32)  10.8 us
    all_to_all x1, blocking collectives, on_device(): lax.all_to_all(gate_here.T[None], 'expert', split_axis=1, concat_axis=0,...  10.2 us
  transfers between devices with their start and end apart: 6, of which 5 were waited for; matrix products, arithmetic and copies ran while one was open for 10% of the time, Pallas kernels for 0%

commit v1 on v0

--- a/solution.py
+++ b/solution.py
@@ -14,7 +14,15 @@
     output = jnp.dot(hidden, second, preferred_element_type=jnp.float32).astype(jnp.bfloat16)
     outs_each, gates_each = (
         lax.all_to_all(output[None], "expert", split_axis=1, concat_axis=0, tiled=True),
-        lax.all_to_all(gate_here.T[None], "expert", split_axis=1, concat_axis=0, tiled=True),
+        jnp.concatenate(
+            lax.all_to_all(
+                jnp.stack(jnp.split(gate_here.T[None], lax.axis_size("expert"), axis=1)),
+                "expert",
+                0,
+                0,
+            ),
+            0,
+        ),
     )
     mixed = jnp.einsum(
         "ert,ero->rto", gates_each, outs_each, preferred_element_type=jnp.float32

time: 472 us -> 476 us (level)
  blocking collectives: 21 us -> 9.82 us
  waiting for transfers between devices: 369 us -> 375 us
  local copies, waits for them, and re-layouts: 12.9 us -> 18.8 us
    all_to_all x2 -> x1, blocking collectives: 21 us -> 9.82 us  [on_device(): lax.all_to_all(jnp.stack(jnp.split(gate_here.T[None], lax.axis_size('expe...]
    all_to_all x0 -> x1, waiting for transfers between devices: none -> 8.13 us  [on_device(): lax.all_to_all(output[None], 'expert', split_axis=1, concat_axis=0, tiled...]
    unnamed x11 -> x18, local copies, waits for them, and re-layouts: 8.85 us -> 14.8 us
  transfers between devices with their start and end apart: 6 -> 7, of which waited for: 5 -> 6; matrix products, arithmetic and copies ran while one was open for 10% -> 11% of each run, Pallas kernels for 0% -> 0%
where the time goes in v1:
time: 476 us; the launch traced here: 475 us
  waiting for transfers between devices  375 us (79%)
  matrix products  44.3 us (9%)
  local copies, waits for them, and re-layouts  18.8 us (4%)
  between operations  13.9 us (3%)
  starting transfers between devices  10.6 us (2%)
  blocking collectives  9.82 us (2%)
    reduce_scatter x1, waiting for transfers between devices, on_device(): lax.psum_scatter(lax.dot_general(piece, d_pre, (((0,), (0,)), ((), ())),...  233 us
    reduce_scatter x1, waiting for transfers between devices, on_device(): lax.psum_scatter(lax.dot_general(piece, d_output, (((0,), (0,)), ((), ())...  79.6 us
    reduce_scatter x1, waiting for transfers between devices, on_device(): lax.psum_scatter(lax.dot_general(piece, first, (((1,), (1,)), ((), ())),...  36.4 us
    unnamed x18, local copies, waits for them, and re-layouts  14.8 us
    all_gather x1, waiting for transfers between devices, on_device(): rows_all = lax.all_gather(trunk, 'expert', axis=0, tiled=True)  13 us
    dot_general x1, matrix products, on_device(): lax.dot_general(piece, first, (((1,), (1,)), ((), ())), preferred_element...  12.6 us
    dot_general x1, matrix products, on_device(): pre = jnp.dot(rows_all, first, preferred_element_type=jnp.float32)  10.8 us
    all_to_all x1, blocking collectives, on_device(): lax.all_to_all(jnp.stack(jnp.split(gate_here.T[None], lax.axis_size('expe...  9.82 us
  transfers between devices with their start and end apart: 7, of which 6 were waited for; matrix products, arithmetic and copies ran while one was open for 11% of the time, Pallas kernels for 0%

profile of v1, /device:TPU:0, one launch (start us, length us, event | category | flops | bytes accessed | tf_op | source)
XLA Modules:
  0.0 474.9 jit_solution(7292121149071244583)
XLA Ops:
  7.9 0.7 constant_dynamic-update-slice_fusion.7
  8.6 0.8 constant_dynamic-update-slice_fusion.6
  9.4 0.8 constant_dynamic-update-slice_fusion.5
  10.1 0.8 constant_dynamic-update-slice_fusion.4
  10.9 0.8 constant_dynamic-update-slice_fusion.3
  11.6 0.8 constant_dynamic-update-slice_fusion.2
  12.4 0.8 constant_dynamic-update-slice_fusion.1
  13.2 0.8 constant_dynamic-update-slice_fusion
  13.9 9.8 %all_to_all.35 = bf16[8,1,24,8]{2,3,1,0:T(8,128)(2,1)S(1)} all-to-all(bf16[8,1,24,8]{2,3,1,0:T(8,128)(2,1)S(1)} %constant_dynamic-update-slice_fusion), channel_id=1, replica_groups=mesh['expert'=8,'dp'=4] {'expert'}, dimensions={0} | all-to-all | bytes 6144 | tf_op jit(solution)/shard_map/all_to_all | solution.py:18
  24.2 1.0 copy.173
  25.1 3.5 all-to-all-start.2
  28.7 13.0 %all-gather.2.cloned.1.call-done = bf16[192,4096]{1,0:T(8,128)(2,1)} async-done(((bf16[24,4096]{1,0:T(8,128)(2,1)}), bf16[192,4096]{1,0:T(8,128)(2,1)}) %all-gather.2.cloned.1.call-update) | async-done | bytes 1572880 | tf_op jit(solution)/shard_map/all_gather | solution.py:8
  41.6 10.8 %fusion.2 = f32[192,2048]{1,0:T(8,128)} fusion(bf16[192,4096]{1,0:T(8,128)(2,1)} %all-gather.2.cloned.1.call-done, bf16[1,4096,2048]{2,1,0:T(8,128)(2,1)} %param.6), kind=kOutput, calls=%fused_computation.2 | convolution fusion | flops 3221225472 | bytes 19922944 | tf_op jit(solution)/shard_map/dot_general | solution.py:12
  52.4 4.5 fusion.17
  57.0 8.1 %convert_bitcast_fusion = bf16[4096,2048]{0,1:T(8,128)(2,1)} fusion(bf16[192,2048]{1,0:T(8,128)(2,1)S(1)} %fusion.17, bf16[192,4096]{1,0:T(8,128)(2,1)S(1)} %copy-done.1), kind=kOutput, calls=%fused_computation.4 | convolution fusion | flops 3229614080 | bytes 19136512 | tf_op jit(solution)/shard_map/dot_general | solution.py:58
  65.2 12.6 %fusion.4 = bf16[192,4096]{1,0:T(8,128)(2,1)} fusion(bf16[192,2048]{1,0:T(8,128)(2,1)S(1)} %fusion.17, bf16[1,4096,2048]{2,1,0:T(8,128)(2,1)} %param.6), kind=kOutput, calls=%fused_computation.5 | convolution fusion | flops 3222011904 | bytes 19136512 | tf_op jit(solution)/shard_map/dot_general | solution.py:49
  78.0 1.2 copy-done.2
  79.2 3.3 convolution_convert_fusion
  82.5 3.2 fusion.24
  86.9 2.9 reduce
  89.8 1.0 reshape.25
  90.8 3.5 all-to-all-start.1
  94.4 8.1 %all-to-all-done.1 = bf16[8,2,12288]{2,1,0:T(2,128)(2,1)S(1)} async-done(((bf16[8,2,12288]{2,1,0:T(2,128)(2,1)}), bf16[8,2,12288]{2,1,0:T(2,128)(2,1)S(1)}, u32[]{:S(2)}, u32[]{:S(2)}) %all-to-all-start.1) | async-done | bytes 393248 | tf_op jit(solution)/shard_map/all_to_all | solution.py:16
  103.4 0.7 copy.175
  104.1 3.3 all-to-all-start.3
  107.4 1.1 convolution_convert_fusion.2
  108.5 3.6 all-to-all-done.3
  112.1 0.7 squeeze.19
  112.8 233.2 %reduce-scatter.6.cloned.1.call-done = bf16[1024,2048]{0,1:T(8,128)(2,1)} async-done(((bf16[4096,2048]{0,1:T(8,128)(2,1)}), bf16[1024,2048]{0,1:T(8,128)(2,1)}) %reduce-scatter.6.cloned.1.call-update) | async-done | bytes 4194320 | tf_op jit(solution)/shard_map/reduce_scatter | solution.py:57
  346.0 6.4 %copy.177 = bf16[1,1024,2048]{2,1,0:T(8,128)(2,1)} copy(bf16[1,1024,2048]{1,2,0:T(8,128)(2,1)} %bitcast.93) | data formatting | bytes 8388608
  352.4 36.4 %reduce-scatter.4.cloned.1.call-done = bf16[24,4096]{1,0:T(8,128)(2,1)} async-done(((bf16[192,4096]{1,0:T(8,128)(2,1)}), bf16[24,4096]{1,0:T(8,128)(2,1)}) %reduce-scatter.4.cloned.1.call-update) | async-done | bytes 196624 | tf_op jit(solution)/shard_map/reduce_scatter | solution.py:48
  388.8 79.6 %reduce-scatter.8.cloned.1.call-done = bf16[512,1024]{1,0:T(8,128)(2,1)} async-done(((bf16[2048,1024]{1,0:T(8,128)(2,1)}), bf16[512,1024]{1,0:T(8,128)(2,1)}) %reduce-scatter.8.cloned.1.call-update) | async-done | bytes 1048592 | tf_op jit(solution)/shard_map/reduce_scatter | solution.py:66
  (23 shorter events, 3.6 us)
Async XLA Ops:
  7.2 16.7 %copy-start = (bf16[24,8,1024]{2,1,0:T(8,128)(2,1)S(1)}, bf16[24,8,1024]{2,1,0:T(8,128)(2,1)}, u32[]{:S(2)}) copy-start(bf16[24,8,1024]{2,1,0:T(8,128)(2,1)} %param.9) | copy-start | bytes 1179652
  7.2 34.4 %all-gather.2.cloned.1.call-start = ((), (), s32[]{:S(2)}) async-start(), calls=%async_computation.7 | async-start | bytes 1769472 | tf_op jit(solution)/shard_map/all_gather | solution.py:8
  25.1 27.3 %all-to-all-start.2 = ((bf16[8,24,1024]{2,1,0:T(8,128)(2,1)}), bf16[8,24,1024]{2,1,0:T(8,128)(2,1)S(1)}, u32[]{:S(2)}, u32[]{:S(2)}) async-start(bf16[8,24,1024]{2,1,0:T(8,128)(2,1)} %copy.173), calls=%async_computation.2 | async-start | bytes 786432 | tf_op jit(solution)/shard_map/all_to_all | solution.py:37
  28.6 317.4 %reduce-scatter.6.cloned.1.call-start = ((), (), s32[]{:S(2)}) async-start(), calls=%async_computation.9 | async-start | bytes 20971520 | tf_op jit(solution)/shard_map/reduce_scatter | solution.py:57
  52.4 4.5 copy-start.1
  65.1 323.7 %reduce-scatter.4.cloned.1.call-start = ((), (), s32[]{:S(2)}) async-start(), calls=%async_computation.8 | async-start | bytes 1769472 | tf_op jit(solution)/shard_map/reduce_scatter | solution.py:48
  77.8 1.4 copy-start.2
  77.8 390.6 %reduce-scatter.8.cloned.1.call-start = ((), (), s32[]{:S(2)}) async-start(), calls=%async_computation.10 | async-start | bytes 5242880 | tf_op jit(solution)/shard_map/reduce_scatter | solution.py:66
  90.8 11.7 %all-to-all-start.1 = ((bf16[8,2,12288]{2,1,0:T(2,128)(2,1)}), bf16[8,2,12288]{2,1,0:T(2,128)(2,1)S(1)}, u32[]{:S(2)}, u32[]{:S(2)}) async-start(bf16[8,2,12288]{2,1,0:T(2,128)(2,1)} %reshape.25), calls=%async_computation.1 | async-start | bytes 786432 | tf_op jit(solution)/shard_map/all_to_all | solution.py:16
  104.1 8.0 %all-to-all-start.3 = ((bf16[8,24,8]{1,2,0:T(8,128)(2,1)}), bf16[8,24,8]{1,2,0:T(8,128)(2,1)S(1)}, u32[]{:S(2)}, u32[]{:S(2)}) async-start(bf16[8,24,8]{1,2,0:T(8,128)(2,1)} %copy.175), calls=%async_computation.4 | async-start | bytes 32768 | tf_op jit(solution)/shard_map/all_to_all | solution.py:38
Sparse Core Ops, SparseCore 0:
  9.9 31.7 all-gather.1
  65.2 280.7 reduce-scatter.5
  349.9 38.9 reduce-scatter.3
  391.5 76.7 reduce-scatter.7
